TPU v7x, 128 devices: a whole 4x4x4 slice. The times are simulated.
128 devices in a mesh: tm: 2 (over core), space: 64 (over z, y, x).
Axes of the slice: x: 4, y: 4, z: 4, core: 2. Of those that a mesh axis runs over, the one named last changes fastest.
Arguments:
- initial: float32 [256, 64, 128], P('space'), may hold values from -6 to 6
- guess: float32 [8, 256, 64, 128], P('tm', 'space'), may hold values from -6 to 6
- conduct: float32 [256, 64, 128], P('space'), may hold values from 0.3 to 3
- source: float32 [256, 64, 128], P('space'), may hold values from -6 to 6
- profile: float32 [64], P('tm'), may hold values from -1 to 1
Outputs:
- corrected: float32 [8, 256, 64, 128], P('tm', 'space')
- residual: float32 [8, 256, 64, 128], P('tm', 'space')
All inputs are finite; a program needn't handle non-finite values.
Results may differ from a plain program's by a relative error of at most 0.000048.
Values sent between devices are 32-bit elements; how exact they have to be, the bound alone decides.
A program may use at most 64 MiB of HBM per device.

v0:
```python
import numpy as np
import jax
import jax.numpy as jnp
from jax import lax
from jax.experimental import pallas as pl
from jax.experimental.pallas import tpu as pltpu
from jax.sharding import PartitionSpec as P

SWEEPS = 3
KAPPA_TOP = 3.0
COARSEN = 8
H = 6
B = 16
LT = B + 2 * H
GROUPS = COARSEN * SWEEPS // H
CH = 3
CT = 4 + 2 * CH
F32 = jnp.float32
MESH = pl.DeviceIdType.MESH


def polynomials(scale, top):
    middle, spread = (top + 1.0) / 2.0, (top - 1.0) / 2.0
    relative = middle / spread
    ratio = 1.0 / relative
    one = np.polynomial.Polynomial([1.0])
    system = np.polynomial.Polynomial([1.0, scale])
    remain = one
    update = remain / middle
    total = update
    for _ in range(SWEEPS - 1):
        remain = remain - system * update
        following = 1.0 / (2.0 * relative - ratio)
        update = following * ratio * update + 2.0 * following / spread * remain
        total = total + update
        ratio = following
    rest = one - np.polynomial.Polynomial([0.0, scale]) * total
    return [float(r) for r in np.sort(rest.roots().real)], [float(c) for c in total.coef]


FINE_ROOTS, FINE_P = polynomials(1.0, 1.0 + 12.0 * KAPPA_TOP)
COARSE_ROOTS, _ = polynomials(float(COARSEN), 1.0 + 12.0 * KAPPA_TOP * COARSEN)


class Masks:
    def __init__(self):
        lane = lax.broadcasted_iota(jnp.int32, (8, 8, 128), 2)
        sub = lax.broadcasted_iota(jnp.int32, (8, 128), 0)
        self.first_lane, self.last_lane = lane == 0, lane == 127
        self.first_sub, self.last_sub = sub == 0, sub == 7


def neighbours(below, centre, above, mk):
    side = jnp.where(mk.first_lane, 0.0, pltpu.roll(centre, 1, 2))
    side = side + jnp.where(mk.last_lane, 0.0, pltpu.roll(centre, 127, 2))
    before = jnp.where(mk.first_sub, 0.0, pltpu.roll(centre[7], 1, 0))
    after = jnp.where(mk.last_sub, 0.0, pltpu.roll(centre[0], 7, 0))
    rows = jnp.concatenate([before[None], centre[:7]], axis=0) + jnp.concatenate(
        [centre[1:], after[None]], axis=0
    )
    return (side + rows) + (below + above)


def natural(ref, layer):
    return jnp.stack([ref[layer, pl.ds(j, 8, stride=8), :] for j in range(8)], axis=0)


def kernel(
    initial, guess, conduct, source, amount,
    corrected, residual,
    nat, con_nat, prof, kap, mul, grow, ua, ub, land, stage, rel, kc, mc, eb, t1, t2, res_in, rel_in,
    in_send, in_recv, nat_send, nat_recv, prof_sem, con_sem, halo_send, halo_recv,
    out_send, out_recv, chain_send, chain_recv,
):
    m = lax.axis_index("tm")
    c = lax.axis_index("space")
    mk = Masks()

    x, y, z = c % 4, (c // 4) % 4, c // 16
    half = y // 2
    s = jnp.where(half == 0, y, 3 - y)
    k = x + 4 * half
    q = 2 * (2 * z + (s + z) % 2) + m

    def device(kk, qq):
        b = qq // 2
        zz = b // 2
        ss = (b % 2 + zz % 2) % 2
        yy = jnp.where(kk // 4 == 0, ss, 3 - ss)
        return (qq % 2, zz * 16 + yy * 4 + kk % 4)

    def remote(src, dst, ssem, rsem, to):
        return pltpu.make_async_remote_copy(
            src_ref=src, dst_ref=dst, send_sem=ssem, recv_sem=rsem, device_id=to, device_id_type=MESH
        )

    def is_me(to):
        return jnp.logical_and(to[0] == m, to[1] == c)

    def push(src, dst, ssem, rsem, to):
        mine = is_me(to)

        @pl.when(mine)
        def _():
            pltpu.make_async_copy(src, dst, rsem).start()

        @pl.when(jnp.logical_not(mine))
        def _():
            remote(src, dst, ssem, rsem, to).start()

    def pushed(src, dst, ssem, rsem, to):
        @pl.when(jnp.logical_not(is_me(to)))
        def _():
            remote(src, dst, ssem, rsem, to).wait_send()

    def arrived(dst, rsem):
        pltpu.make_async_copy(dst, dst, rsem).wait()

    sq, sr = c // 4, c % 4
    place = pl.ds(H + 4 * sr, 4)
    own = pl.ds(H, B)
    sends = []

    def give(array, slot, src, kk, when=None):
        args = (src, nat.at[array, place], in_send.at[array, slot], in_recv.at[array, sr], device(kk, sq))
        sends.append((args, when))
        if when is None:
            push(*args)
        else:
            pl.when(when)(lambda: push(*args))

    chain_left, chain_right = (m, c - 1), (m, c + 1)
    has_cl, has_cr = c > 0, c < 63
    con_local = pltpu.make_async_copy(conduct, con_nat.at[pl.ds(CH, 4)], con_sem.at[0])
    to_cl = remote(conduct.at[pl.ds(0, CH)], con_nat.at[pl.ds(CH + 4, CH)], con_sem.at[1], con_sem.at[2], chain_left)
    to_cr = remote(conduct.at[pl.ds(1, CH)], con_nat.at[pl.ds(0, CH)], con_sem.at[3], con_sem.at[4], chain_right)

    partner = (1 - m, c)
    to_partner = remote(amount, prof.at[pl.ds(4 * m, 4)], prof_sem.at[0], prof_sem.at[1], partner)
    mine_prof = pltpu.make_async_copy(amount, prof.at[pl.ds(4 * m, 4)], prof_sem.at[2])

    for i in range(4):
        give(0, i, conduct, 4 * m + i)
    pl.when(m == 0)(lambda: push(initial, nat.at[1, place], in_send.at[1, 4], in_recv.at[1, sr], device(0, sq)))
    for i in range(3):
        give(1, i, guess.at[i], 4 * m + i + 1)
    give(1, 3, guess.at[3], 4, m == 0)
    for i in range(4):
        give(2, i, source, 4 * m + i)
    to_partner.start()
    mine_prof.start()
    for i in range(3):
        give(3, i, guess.at[i], 4 * m + i)
    give(3, 3, guess.at[3], 3, m == 0)
    pl.when(m == 1)(lambda: push(initial, nat.at[3, place], in_send.at[3, 4], in_recv.at[3, sr], device(7, sq)))
    con_local.start()
    pl.when(has_cl)(lambda: to_cl.start())
    pl.when(has_cr)(lambda: to_cr.start())

    left, right = device(k, jnp.maximum(q - 1, 0)), device(k, jnp.minimum(q + 1, 15))
    has_l, has_r = q > 0, q < 15
    nat_copies = []
    for array in range(3):
        to_l = remote(
            nat.at[array, pl.ds(H, H)], nat.at[array, pl.ds(H + B, H)],
            nat_send.at[0, array], nat_recv.at[0, array], left,
        )
        to_r = remote(
            nat.at[array, pl.ds(B, H)], nat.at[array, pl.ds(0, H)],
            nat_send.at[1, array], nat_recv.at[1, array], right,
        )
        nat_copies.append((to_l, to_r))
        for r in range(2):
            arrived(nat.at[array, pl.ds(H + 4 * r, 4)], in_recv.at[array, r])
        pl.when(has_l)(lambda: to_l.start())
        for r in range(2, 4):
            arrived(nat.at[array, pl.ds(H + 4 * r, 4)], in_recv.at[array, r])
        pl.when(has_r)(lambda: to_r.start())

    def halo_arrived(array):
        pl.when(has_r)(lambda: arrived(nat.at[array, pl.ds(H + B, H)], nat_recv.at[0, array]))
        pl.when(has_l)(lambda: arrived(nat.at[array, pl.ds(0, H)], nat_recv.at[1, array]))

    def coefficients(layer, cond):
        for n in range(3):
            kappa = cond * (1.0 / FINE_ROOTS[n])
            kap[n, layer] = kappa
            mul[n, layer] = 1.0 - 6.0 * kappa
        kap[3, layer] = cond

    nothing = jnp.zeros((8, 8, 128), F32)

    def edges(has, first, fill, blank):
        @pl.when(has)
        def _():
            @pl.loop(first, first + H)
            def _(layer):
                fill(layer)

        @pl.when(jnp.logical_not(has))
        def _():
            @pl.loop(first, first + H)
            def _(layer):
                blank(layer)

    def fill_con(layer):
        coefficients(layer, natural(nat.at[0], layer))

    def blank_con(layer):
        for n in range(3):
            kap[n, layer] = nothing
            mul[n, layer] = nothing
        kap[3, layer] = nothing

    def fill_src(layer):
        ub[layer] = natural(nat.at[2], layer)

    def blank_src(layer):
        ub[layer] = nothing

    @pl.loop(H, H + B)
    def _(layer):
        fill_con(layer)

    halo_arrived(0)
    edges(has_l, 0, fill_con, blank_con)
    edges(has_r, H + B, fill_con, blank_con)

    @pl.loop(H, H + B)
    def _(layer):
        fill_src(layer)

    halo_arrived(2)
    edges(has_l, 0, fill_src, blank_src)
    edges(has_r, H + B, fill_src, blank_src)

    def applied(ref, layer):
        centre = ref[layer]
        return kap[3, layer] * (6.0 * centre - neighbours(ref[layer - 1], centre, ref[layer + 1], mk))

    @pl.loop(1, LT - 1)
    def _(layer):
        ua[layer] = FINE_P[1] * ub[layer] + FINE_P[2] * applied(ub, layer)

    @pl.loop(2, LT - 2)
    def _(layer):
        grow[layer] = FINE_P[0] * ub[layer] + applied(ua, layer)

    @pl.loop(H, H + B)
    def _(layer):
        ua[layer] = natural(nat.at[1], layer)

    halo_arrived(1)
    for side, has, first in ((0, has_l, 0), (1, has_r, H + B)):
        def fill(layer, side=side, first=first):
            land[0, side, layer - first] = natural(nat.at[1], layer)

        def blank(layer, side=side, first=first):
            land[0, side, layer - first] = nothing
            land[1, side, layer - first] = nothing

        edges(has, first, fill, blank)

    arrived(prof.at[pl.ds(4 * (1 - m), 4)], prof_sem.at[1])
    mine_prof.wait()

    def state_copies(t):
        p = t % 2
        return (
            remote(stage.at[p, 0], land.at[p, 1], halo_send.at[0, p], halo_recv.at[0, p], left),
            remote(stage.at[p, 1], land.at[p, 0], halo_send.at[1, p], halo_recv.at[1, p], right),
        )

    def group(g, with_source):
        parity = g % 2
        following = (g + 1) % 2
        bufs = (ua, ub)

        def read(i, layer):
            if i == 0 and layer < H:
                return land[parity, 0, layer]
            if i == 0 and layer >= H + B:
                return land[parity, 1, layer - H - B]
            return bufs[i % 2][layer]

        amounts = {}
        if with_source:
            for n in range(H // 3):
                row = prof[k, pl.ds(g * (H // 3) + n, 1), :]
                amounts[3 * n + 3] = jnp.broadcast_to(row, (8, 128))

        def region(bounds, sent=None):
            todo = []
            for i in range(1, H + 1):
                lo, hi = bounds(i)
                todo += [(layer + 2 * i, i, layer) for layer in range(lo, hi)]
            for _, i, layer in sorted(todo):
                n = (i - 1) % 3
                centre = read(i - 1, layer)
                total = neighbours(read(i - 1, layer - 1), centre, read(i - 1, layer + 1), mk)
                value = mul[n, layer] * centre + kap[n, layer] * total
                if i in amounts:
                    value = value + amounts[i][None] * grow[layer]
                bufs[i % 2][layer] = value
                if i == H and sent is not None:
                    stage[following, sent[0], layer - sent[1]] = value

        @pl.when(g >= 2)
        def _():
            a, b = state_copies(g + 1)
            pl.when(has_l)(lambda: a.wait_send())
            pl.when(has_r)(lambda: b.wait_send())

        region(lambda i: (H + i, H + B - i))
        a, b = state_copies(g)
        c_, d_ = state_copies(g + 1)
        last = COARSEN * SWEEPS // H

        @pl.when(jnp.logical_and(g > 0, has_l))
        def _():
            b.wait_recv()

        region(lambda i: (i, H + i), (0, H))

        @pl.when(jnp.logical_and((g + 1) % last != 0, has_l))
        def _():
            c_.start()

        @pl.when(jnp.logical_and(g > 0, has_r))
        def _():
            a.wait_recv()

        region(lambda i: (LT - H - i, LT - i), (1, B))

        @pl.when(jnp.logical_and((g + 1) % last != 0, has_r))
        def _():
            d_.start()

    @pl.loop(0, GROUPS)
    def _(g):
        group(g, True)

    for r in range(4):
        arrived(nat.at[3, pl.ds(H + 4 * r, 4)], in_recv.at[3, r])
    first_copies = state_copies(GROUPS)
    final = k == 7

    def difference(layer):
        value = ua[layer]
        off = natural(nat.at[3], layer)
        rel[layer - H] = value
        value = jnp.where(final, off, value) - off
        ua[layer] = value
        return value

    @pl.loop(0, H)
    def _(i):
        stage[GROUPS % 2, 0, i] = difference(H + i)

    pl.when(has_l)(lambda: first_copies[0].start())

    @pl.loop(2 * H, B)
    def _(layer):
        difference(layer)

    @pl.loop(0, H)
    def _(i):
        stage[GROUPS % 2, 1, i] = difference(B + i)

    pl.when(has_r)(lambda: first_copies[1].start())

    after = (k + 1) % 8
    rel_args = [
        (rel.at[pl.ds(4 * r, 4)], rel_in.at[k % 4], out_send.at[0, r], out_recv.at[0, k % 4], (k // 4, 4 * q + r))
        for r in range(4)
    ]
    res_args = [
        (ua.at[pl.ds(H + 4 * r, 4)], res_in.at[after % 4], out_send.at[1, r], out_recv.at[1, after % 4], (after // 4, 4 * q + r))
        for r in range(4)
    ]
    for args in rel_args:
        push(*args)

    @pl.loop(GROUPS, 2 * GROUPS)
    def _(g):
        group(g, False)

    for args in res_args:
        push(*args)

    con_local.wait()
    pl.when(has_cl)(lambda: to_cr.wait_recv())
    pl.when(has_cr)(lambda: to_cl.wait_recv())

    def chain_fill(layer):
        cond = natural(con_nat, layer)
        for n in range(3):
            kappa = cond * (1.0 / COARSE_ROOTS[n])
            kc[n, layer] = kappa
            mc[n, layer] = 1.0 - 6.0 * kappa

    for layer in range(CH, CH + 4):
        chain_fill(layer)
    for has, first in ((has_cl, 0), (has_cr, CH + 4)):
        @pl.when(has)
        def _(first=first):
            for layer in range(first, first + CH):
                chain_fill(layer)

        @pl.when(jnp.logical_not(has))
        def _(first=first):
            for layer in range(first, first + CH):
                for n in range(3):
                    kc[n, layer] = nothing
                    mc[n, layer] = nothing
                eb[0, layer] = nothing
                eb[1, layer] = nothing

    def out_rows(ref, i, layer, value):
        for j in range(8):
            ref[i, layer, pl.ds(j, 8, stride=8), :] = value[j]

    def chain_copies(i):
        p = i % 2
        core = jnp.where(i == 3, 1, m)
        lft, rgt = (core, c - 1), (core, c + 1)
        return (
            remote(eb.at[p, pl.ds(CH, CH)], eb.at[p, pl.ds(CH + 4, CH)], chain_send.at[0, p], chain_recv.at[0, p], lft),
            remote(eb.at[p, pl.ds(4, CH)], eb.at[p, pl.ds(0, CH)], chain_send.at[1, p], chain_recv.at[1, p], rgt),
        )

    over = remote(eb.at[1, pl.ds(CH, 4)], eb.at[1, pl.ds(CH, 4)], chain_send.at[2, 0], chain_recv.at[2, 0], (1, c))

    @pl.loop(0, 4)
    def _(i):
        p = i % 2
        o = 1 - p
        arrived(res_in.at[i], out_recv.at[1, i])
        start = jnp.logical_and(m == 0, i == 0)

        @pl.when(start)
        def _():
            for layer in range(4):
                eb[p, CH + layer] = res_in[i, layer]

        @pl.when(jnp.logical_not(start))
        def _():
            a, b = chain_copies(i + 1)
            pl.when(has_cr)(lambda: a.wait_recv())
            pl.when(has_cl)(lambda: b.wait_recv())
            pl.when(i == 0)(lambda: over.wait_recv())

            @pl.when(i >= 2)
            def _():
                d, e = chain_copies(i - 2)
                pl.when(has_cl)(lambda: d.wait_send())
                pl.when(has_cr)(lambda: e.wait_send())

            src = eb.at[o]
            for n, dst in enumerate((t1, t2, None)):
                for layer in range(n + 1, CT - n - 1):
                    centre = src[layer]
                    total = neighbours(src[layer - 1], centre, src[layer + 1], mk)
                    value = mc[n, layer] * centre + kc[n, layer] * total
                    if dst is None:
                        eb[p, layer] = value + res_in[i, layer - CH]
                    else:
                        dst[layer] = value
                src = dst

        d, e = chain_copies(i)
        more = jnp.logical_or(i < 3, m == 0)
        pl.when(jnp.logical_and(more, has_cl))(lambda: d.start())
        pl.when(jnp.logical_and(more, has_cr))(lambda: e.start())
        pl.when(jnp.logical_and(i == 3, m == 0))(lambda: over.start())
        arrived(rel_in.at[i], out_recv.at[0, i])
        for layer in range(4):
            out_rows(residual, i, layer, res_in[i, layer])
            out_rows(corrected, i, layer, rel_in[i, layer] + eb[p, CH + layer])

    d, e = chain_copies(2)
    pl.when(has_cl)(lambda: d.wait_send())
    pl.when(has_cr)(lambda: e.wait_send())
    d, e = chain_copies(3)

    @pl.when(m == 0)
    def _():
        pl.when(has_cl)(lambda: d.wait_send())
        pl.when(has_cr)(lambda: e.wait_send())
        over.wait_send()

    for args, when in sends:
        if when is None:
            pushed(*args)
        else:
            pl.when(when)(lambda: pushed(*args))
    pl.when(m == 0)(lambda: pushed(initial, nat.at[1, place], in_send.at[1, 4], in_recv.at[1, sr], device(0, sq)))
    pl.when(m == 1)(lambda: pushed(initial, nat.at[3, place], in_send.at[3, 4], in_recv.at[3, sr], device(7, sq)))
    for to_l, to_r in nat_copies:
        pl.when(has_l)(lambda: to_l.wait_send())
        pl.when(has_r)(lambda: to_r.wait_send())
    pl.when(has_cl)(lambda: to_cl.wait_send())
    pl.when(has_cr)(lambda: to_cr.wait_send())
    to_partner.wait_send()
    for args in rel_args + res_args:
        pushed(*args)
    a, b = state_copies(2 * GROUPS - 1)
    pl.when(has_l)(lambda: a.wait_send())
    pl.when(has_r)(lambda: b.wait_send())


def body(initial, guess, conduct, source, profile):
    amount = jnp.broadcast_to(profile.reshape(4, COARSEN, 1), (4, COARSEN, 128))
    anyspace = pl.BlockSpec(memory_space=pl.ANY)
    vmem = pl.BlockSpec(memory_space=pltpu.VMEM)
    out = jax.ShapeDtypeStruct((4, 4, 64, 128), F32)
    dma = pltpu.SemaphoreType.DMA

    def layers(*lead):
        return pltpu.VMEM((*lead, 8, 8, 128), F32)

    return pl.pallas_call(
        kernel,
        name="mgrit",
        out_shape=(out, out),
        in_specs=[anyspace, anyspace, anyspace, anyspace, vmem],
        out_specs=(vmem, vmem),
        scratch_shapes=[
            pltpu.VMEM((4, LT, 64, 128), F32),
            pltpu.VMEM((CT, 64, 128), F32),
            pltpu.VMEM((8, COARSEN, 128), F32),
            layers(4, LT),
            layers(3, LT),
            layers(LT),
            layers(LT),
            layers(LT),
            layers(2, 2, H),
            layers(2, 2, H),
            layers(B),
            layers(3, CT),
            layers(3, CT),
            layers(2, CT),
            layers(CT),
            layers(CT),
            layers(4, 4),
            layers(4, 4),
            dma((4, 5)), dma((4, 4)),
            dma((2, 3)), dma((2, 3)),
            dma((3,)), dma((5,)),
            dma((2, 2)), dma((2, 2)),
            dma((2, 4)), dma((2, 4)),
            dma((3, 2)), dma((3, 2)),
        ],
        compiler_params=pltpu.CompilerParams(has_side_effects=True, vmem_limit_bytes=48 * 1024 * 1024),
    )(initial, guess, conduct, source, amount)


def solution(mesh):
    return jax.shard_map(
        body,
        mesh=mesh,
        in_specs=(
            P("space", None, None),
            P("tm", "space", None, None),
            P("space", None, None),
            P("space", None, None),
            P("tm"),
        ),
        out_specs=(P("tm", "space", None, None), P("tm", "space", None, None)),
        check_vma=False,
    )
```

profile of v0, /device:TPU:31, one launch (start us, length us, event | category | flops | bytes accessed | tf_op | source)
XLA Modules:
  0.0 174.4 jit_solution(13214571076560840526)
XLA Ops:
  0.6 0.7 broadcast_in_dim.7
  1.4 0.1 broadcast_in_dim.8.amount
  1.4 0.0 copy-start
  1.4 1.0 copy-done
  2.5 0.0 copy-start.1
  2.5 0.9 copy-done.1
  3.4 0.0 copy-start.2
  3.4 0.9 copy-done.2
  4.3 0.0 copy-start.3
  4.3 0.9 copy-done.3
  5.2 167.6 %mgrit.1 = (f32[4,4,64,128]{3,2,1,0:T(8,128)S(1)}, f32[4,4,64,128]{3,2,1,0:T(8,128)S(1)}) custom-call(f32[4,64,128]{2,1,0:T(8,128)S(1)} %copy-done.1, f32[4,4,64,128]{3,2,1,0:T(8,128)S(1)} %copy-done, f32[4,64,128]{2,1,0:T(8,128)S(1)} %copy-done.2, f32[4,64,128]{2,1,0:T(8,128)S(1)} %copy-done.3, f32[4,8,128]{2,1,0:T(8,128)S(1)} %broadcast_in_dim.8.amount), custom_call_target="tpu_custom_call" | custom-call | tf_op jit(solution)/shard_map/mgrit/pallas_call | solution.py:522
  172.8 0.8 copy.9
  173.6 0.8 copy.10
Async XLA Ops:
  1.4 1.0 copy-start
  2.5 0.9 copy-start.1
  3.4 0.9 copy-start.2
  4.3 0.9 copy-start.3
where the time goes:
time: 175 us; the launch traced here: 174 us
  Pallas kernels  168 us (96%)
  local copies, waits for them, and re-layouts  6.15 us (4%)
    pallas_call x1, Pallas kernels, body(): pl.pallas_call(kernel, name='mgrit', out_shape=(out, out), in_specs=[anys...  168 us
    unnamed x10, local copies, waits for them, and re-layouts  5.34 us

commit v1 on v0

--- a/solution.py
+++ b/solution.py
@@ -69,7 +69,7 @@
     initial, guess, conduct, source, amount,
     corrected, residual,
     nat, con_nat, prof, kap, mul, grow, ua, ub, land, stage, rel, kc, mc, eb, t1, t2, res_in, rel_in,
-    in_send, in_recv, nat_send, nat_recv, prof_sem, con_sem, halo_send, halo_recv,
+    in_send, in_recv, nat_send, nat_recv, prof_sem, con_sem, sub_sem, halo_send, halo_recv,
     out_send, out_recv, chain_send, chain_recv,
 ):
     m = lax.axis_index("tm")
@@ -116,7 +116,10 @@
     def arrived(dst, rsem):
         pltpu.make_async_copy(dst, dst, rsem).wait()
 
+    left, right = device(k, jnp.maximum(q - 1, 0)), device(k, jnp.minimum(q + 1, 15))
+    has_l, has_r = q > 0, q < 15
     sq, sr = c // 4, c % 4
+    has_cl, has_cr = c > 0, c < 63
     place = pl.ds(H + 4 * sr, 4)
     own = pl.ds(H, B)
     sends = []
@@ -130,37 +133,33 @@
             pl.when(when)(lambda: push(*args))
 
     chain_left, chain_right = (m, c - 1), (m, c + 1)
-    has_cl, has_cr = c > 0, c < 63
     con_local = pltpu.make_async_copy(conduct, con_nat.at[pl.ds(CH, 4)], con_sem.at[0])
     to_cl = remote(conduct.at[pl.ds(0, CH)], con_nat.at[pl.ds(CH + 4, CH)], con_sem.at[1], con_sem.at[2], chain_left)
     to_cr = remote(conduct.at[pl.ds(1, CH)], con_nat.at[pl.ds(0, CH)], con_sem.at[3], con_sem.at[4], chain_right)
 
     partner = (1 - m, c)
-    to_partner = remote(amount, prof.at[pl.ds(4 * m, 4)], prof_sem.at[0], prof_sem.at[1], partner)
-    mine_prof = pltpu.make_async_copy(amount, prof.at[pl.ds(4 * m, 4)], prof_sem.at[2])
-
-    for i in range(4):
-        give(0, i, conduct, 4 * m + i)
+    to_partner = remote(amount, prof.at[m], prof_sem.at[0], prof_sem.at[1], partner)
+
+    give(0, 0, conduct, x + 4 * m)
+    give(2, 0, source, x + 4 * m)
+    relays = {}
+    for array in (0, 2):
+        column = nat.at[array, pl.ds(H + 4 * x, 4)]
+        relays[array] = [
+            remote(column, column, in_send.at[array, d], in_recv.at[array, x], (m, 16 * z + 4 * y + (x + d) % 4)) for d in range(1, 4)
+        ]
+        arrived(column, in_recv.at[array, x])
+        for relay in relays[array]:
+            relay.start()
     pl.when(m == 0)(lambda: push(initial, nat.at[1, place], in_send.at[1, 4], in_recv.at[1, sr], device(0, sq)))
     for i in range(3):
         give(1, i, guess.at[i], 4 * m + i + 1)
     give(1, 3, guess.at[3], 4, m == 0)
-    for i in range(4):
-        give(2, i, source, 4 * m + i)
-    to_partner.start()
-    mine_prof.start()
-    for i in range(3):
-        give(3, i, guess.at[i], 4 * m + i)
-    give(3, 3, guess.at[3], 3, m == 0)
-    pl.when(m == 1)(lambda: push(initial, nat.at[3, place], in_send.at[3, 4], in_recv.at[3, sr], device(7, sq)))
-    con_local.start()
-    pl.when(has_cl)(lambda: to_cl.start())
-    pl.when(has_cr)(lambda: to_cr.start())
-
-    left, right = device(k, jnp.maximum(q - 1, 0)), device(k, jnp.minimum(q + 1, 15))
-    has_l, has_r = q > 0, q < 15
+    prof[m] = amount[...]
+
     nat_copies = []
-    for array in range(3):
+
+    def beside(array):
         to_l = remote(
             nat.at[array, pl.ds(H, H)], nat.at[array, pl.ds(H + B, H)],
             nat_send.at[0, array], nat_recv.at[0, array], left,
@@ -170,11 +169,21 @@
             nat_send.at[1, array], nat_recv.at[1, array], right,
         )
         nat_copies.append((to_l, to_r))
-        for r in range(2):
-            arrived(nat.at[array, pl.ds(H + 4 * r, 4)], in_recv.at[array, r])
+
+        def piece(r):
+            def come():
+                arrived(nat.at[array, pl.ds(H + 4 * r, 4)], in_recv.at[array, r])
+
+            if array == 1:
+                come()
+            else:
+                pl.when(x != r)(come)
+
+        piece(0)
+        piece(1)
         pl.when(has_l)(lambda: to_l.start())
-        for r in range(2, 4):
-            arrived(nat.at[array, pl.ds(H + 4 * r, 4)], in_recv.at[array, r])
+        piece(2)
+        piece(3)
         pl.when(has_r)(lambda: to_r.start())
 
     def halo_arrived(array):
@@ -218,10 +227,13 @@
     def blank_src(layer):
         ub[layer] = nothing
 
+    beside(0)
+
     @pl.loop(H, H + B)
     def _(layer):
         fill_con(layer)
 
+    beside(2)
     halo_arrived(0)
     edges(has_l, 0, fill_con, blank_con)
     edges(has_r, H + B, fill_con, blank_con)
@@ -245,6 +257,15 @@
     @pl.loop(2, LT - 2)
     def _(layer):
         grow[layer] = FINE_P[0] * ub[layer] + applied(ua, layer)
+
+    beside(1)
+    sub_src, sub_dst = nat.at[1, own], nat.at[3, own]
+    sub = remote(sub_src, sub_dst, sub_sem.at[0], sub_sem.at[1], device((k + 7) % 8, q))
+    sub.start()
+    con_local.start()
+    to_partner.start()
+    pl.when(has_cl)(lambda: to_cl.start())
+    pl.when(has_cr)(lambda: to_cr.start())
 
     @pl.loop(H, H + B)
     def _(layer):
@@ -261,8 +282,7 @@
 
         edges(has, first, fill, blank)
 
-    arrived(prof.at[pl.ds(4 * (1 - m), 4)], prof_sem.at[1])
-    mine_prof.wait()
+    arrived(prof.at[1 - m], prof_sem.at[1])
 
     def state_copies(t):
         p = t % 2
@@ -286,7 +306,7 @@
         amounts = {}
         if with_source:
             for n in range(H // 3):
-                row = prof[k, pl.ds(g * (H // 3) + n, 1), :]
+                row = prof[k // 4, pl.ds(COARSEN * (k % 4) + g * (H // 3) + n, 1), :]
                 amounts[3 * n + 3] = jnp.broadcast_to(row, (8, 128))
 
         def region(bounds, sent=None):
@@ -340,8 +360,7 @@
     def _(g):
         group(g, True)
 
-    for r in range(4):
-        arrived(nat.at[3, pl.ds(H + 4 * r, 4)], in_recv.at[3, r])
+    arrived(sub_dst, sub_sem.at[1])
     first_copies = state_copies(GROUPS)
     final = k == 7
 
@@ -495,7 +514,10 @@
         else:
             pl.when(when)(lambda: pushed(*args))
     pl.when(m == 0)(lambda: pushed(initial, nat.at[1, place], in_send.at[1, 4], in_recv.at[1, sr], device(0, sq)))
-    pl.when(m == 1)(lambda: pushed(initial, nat.at[3, place], in_send.at[3, 4], in_recv.at[3, sr], device(7, sq)))
+    for array in (0, 2):
+        for relay in relays[array]:
+            relay.wait_send()
+    sub.wait_send()
     for to_l, to_r in nat_copies:
         pl.when(has_l)(lambda: to_l.wait_send())
         pl.when(has_r)(lambda: to_r.wait_send())
@@ -510,7 +532,7 @@
 
 
 def body(initial, guess, conduct, source, profile):
-    amount = jnp.broadcast_to(profile.reshape(4, COARSEN, 1), (4, COARSEN, 128))
+    amount = jnp.broadcast_to(profile[:, None], (4 * COARSEN, 128))
     anyspace = pl.BlockSpec(memory_space=pl.ANY)
     vmem = pl.BlockSpec(memory_space=pltpu.VMEM)
     out = jax.ShapeDtypeStruct((4, 4, 64, 128), F32)
@@ -528,7 +550,7 @@
         scratch_shapes=[
             pltpu.VMEM((4, LT, 64, 128), F32),
             pltpu.VMEM((CT, 64, 128), F32),
-            pltpu.VMEM((8, COARSEN, 128), F32),
+            pltpu.VMEM((2, 4 * COARSEN, 128), F32),
             layers(4, LT),
             layers(3, LT),
             layers(LT),
@@ -546,12 +568,14 @@
             layers(4, 4),
             dma((4, 5)), dma((4, 4)),
             dma((2, 3)), dma((2, 3)),
-            dma((3,)), dma((5,)),
+            dma((2,)), dma((5,)), dma((2,)),
             dma((2, 2)), dma((2, 2)),
             dma((2, 4)), dma((2, 4)),
             dma((3, 2)), dma((3, 2)),
         ],
-        compiler_params=pltpu.CompilerParams(has_side_effects=True, vmem_limit_bytes=48 * 1024 * 1024),
+        compiler_params=pltpu.CompilerParams(
+            has_side_effects=True, vmem_limit_bytes=67043328
+        ),
     )(initial, guess, conduct, source, amount)
 
 

time: 175 us -> 146 us (0.83)
  the two profiles are of different devices: /device:TPU:31 before, /device:TPU:65 now
where the time goes in v1:
time: 146 us
  Pallas kernels  141 us (97%)
  local copies, waits for them, and re-layouts  4.07 us (3%)
    pallas_call x1, Pallas kernels, body(): pl.pallas_call(kernel, name='mgrit', out_shape=(out, out), in_specs=[anys...  141 us

profile of v1, /device:TPU:65, one launch (start us, length us, event | category | flops | bytes accessed | tf_op | source)
XLA Modules:
  0.0 145.7 jit_solution(14291674574217091320)
XLA Ops:
  0.6 1.3 broadcast_in_dim.2.amount
  2.0 141.0 %mgrit.1 = (f32[4,4,64,128]{3,2,1,0:T(8,128)}, f32[4,4,64,128]{3,2,1,0:T(8,128)}) custom-call(f32[4,64,128]{2,1,0:T(8,128)} %initial.1, f32[4,4,64,128]{3,2,1,0:T(8,128)} %guess.1, f32[4,64,128]{2,1,0:T(8,128)} %conduct.1, f32[4,64,128]{2,1,0:T(8,128)} %source.1, f32[32,128]{1,0:T(8,128)} %broadcast_in_dim.2.amount), custom_call_target="tpu_custom_call" | custom-call | tf_op jit(solution)/shard_map/mgrit/pallas_call | solution.py:544
  142.9 0.0 copy-start
  142.9 1.9 %copy.9 = f32[4,4,64,128]{3,2,1,0:T(8,128)} copy(f32[4,4,64,128]{3,2,1,0:T(8,128)} %get-tuple-element.4) | data formatting | bytes 1048576
  144.9 0.0 copy-done
  144.9 0.8 copy.10
Async XLA Ops:
  142.9 2.0 %copy-start = (f32[4,4,64,128]{3,2,1,0:T(8,128)S(1)}, f32[4,4,64,128]{3,2,1,0:T(8,128)}, u32[]{:S(2)}) copy-start(f32[4,4,64,128]{3,2,1,0:T(8,128)} %get-tuple-element.5) | copy-start | bytes 1572868

commit v2 on v1

--- a/solution.py
+++ b/solution.py
@@ -120,6 +120,24 @@
     has_l, has_r = q > 0, q < 15
     sq, sr = c // 4, c % 4
     has_cl, has_cr = c > 0, c < 63
+    barrier = pltpu.get_barrier_semaphore()
+
+    def hello(to):
+        pl.semaphore_signal(barrier, inc=1, device_id=to, device_id_type=MESH)
+
+    for kk in range(8):
+        for to in (device(kk, sq), (kk // 4, 4 * q + kk % 4)):
+            pl.when(jnp.logical_not(is_me(to)))(lambda: hello(to))
+    for d in range(1, 8):
+        hello(device((k + d) % 8, q))
+    hello((1 - m, c))
+    hello(device(k, (q + 1) % 16))
+    hello(device(k, (q + 15) % 16))
+    for d in (1, 63):
+        hello((0, (c + d) % 64))
+        hello((1, (c + d) % 64))
+    pl.semaphore_wait(barrier, 30 - 2 * jnp.where(sq == q, 1, 0))
+
     place = pl.ds(H + 4 * sr, 4)
     own = pl.ds(H, B)
     sends = []
@@ -574,7 +592,7 @@
             dma((3, 2)), dma((3, 2)),
         ],
         compiler_params=pltpu.CompilerParams(
-            has_side_effects=True, vmem_limit_bytes=67043328
+            collective_id=0, has_side_effects=True, vmem_limit_bytes=67043328
         ),
     )(initial, guess, conduct, source, amount)
 

time: 146 us -> 137 us (0.938)
  the two profiles are of different devices: /device:TPU:65 before, /device:TPU:31 now
where the time goes in v2:
time: 137 us
  Pallas kernels  132 us (96%)
  local copies, waits for them, and re-layouts  4.07 us (3%)
    pallas_call x1, Pallas kernels, body(): pl.pallas_call(kernel, name='mgrit', out_shape=(out, out), in_specs=[anys...  132 us

profile of v2, /device:TPU:31, one launch (start us, length us, event | category | flops | bytes accessed | tf_op | source)
XLA Modules:
  0.0 136.5 jit_solution(12615242619637954190)
XLA Ops:
  0.6 1.3 broadcast_in_dim.2.amount
  2.0 131.8 %mgrit.1 = (f32[4,4,64,128]{3,2,1,0:T(8,128)}, f32[4,4,64,128]{3,2,1,0:T(8,128)}) custom-call(f32[4,64,128]{2,1,0:T(8,128)} %initial.1, f32[4,4,64,128]{3,2,1,0:T(8,128)} %guess.1, f32[4,64,128]{2,1,0:T(8,128)} %conduct.1, f32[4,64,128]{2,1,0:T(8,128)} %source.1, f32[32,128]{1,0:T(8,128)} %broadcast_in_dim.2.amount), custom_call_target="tpu_custom_call" | custom-call | tf_op jit(solution)/shard_map/mgrit/pallas_call | solution.py:562
  133.8 0.0 copy-start
  133.8 1.9 %copy.9 = f32[4,4,64,128]{3,2,1,0:T(8,128)} copy(f32[4,4,64,128]{3,2,1,0:T(8,128)} %get-tuple-element.4) | data formatting | bytes 1048576
  135.7 0.0 copy-done
  135.7 0.8 copy.10
Async XLA Ops:
  133.8 2.0 %copy-start = (f32[4,4,64,128]{3,2,1,0:T(8,128)S(1)}, f32[4,4,64,128]{3,2,1,0:T(8,128)}, u32[]{:S(2)}) copy-start(f32[4,4,64,128]{3,2,1,0:T(8,128)} %get-tuple-element.5) | copy-start | bytes 1572868

commit v3 on v2

--- a/solution.py
+++ b/solution.py
@@ -65,12 +65,21 @@
     return jnp.stack([ref[layer, pl.ds(j, 8, stride=8), :] for j in range(8)], axis=0)
 
 
+def each(lo, hi, run, unroll):
+    assert (hi - lo) % unroll == 0
+
+    @pl.loop(0, (hi - lo) // unroll)
+    def _(t):
+        for d in range(unroll):
+            run(lo + t * unroll + d)
+
+
 def kernel(
     initial, guess, conduct, source, amount,
     corrected, residual,
     nat, con_nat, prof, kap, mul, grow, ua, ub, land, stage, rel, kc, mc, eb, t1, t2, res_in, rel_in,
     in_send, in_recv, nat_send, nat_recv, prof_sem, con_sem, sub_sem, halo_send, halo_recv,
-    out_send, out_recv, chain_send, chain_recv,
+    out_send, out_recv, chain_send, chain_recv, turn,
 ):
     m = lax.axis_index("tm")
     c = lax.axis_index("space")
@@ -220,15 +229,11 @@
     def edges(has, first, fill, blank):
         @pl.when(has)
         def _():
-            @pl.loop(first, first + H)
-            def _(layer):
-                fill(layer)
+            each(first, first + H, fill, 3)
 
         @pl.when(jnp.logical_not(has))
         def _():
-            @pl.loop(first, first + H)
-            def _(layer):
-                blank(layer)
+            each(first, first + H, blank, 3)
 
     def fill_con(layer):
         coefficients(layer, natural(nat.at[0], layer))
@@ -247,35 +252,9 @@
 
     beside(0)
 
-    @pl.loop(H, H + B)
-    def _(layer):
-        fill_con(layer)
+    each(H, H + B, fill_con, 4)
 
     beside(2)
-    halo_arrived(0)
-    edges(has_l, 0, fill_con, blank_con)
-    edges(has_r, H + B, fill_con, blank_con)
-
-    @pl.loop(H, H + B)
-    def _(layer):
-        fill_src(layer)
-
-    halo_arrived(2)
-    edges(has_l, 0, fill_src, blank_src)
-    edges(has_r, H + B, fill_src, blank_src)
-
-    def applied(ref, layer):
-        centre = ref[layer]
-        return kap[3, layer] * (6.0 * centre - neighbours(ref[layer - 1], centre, ref[layer + 1], mk))
-
-    @pl.loop(1, LT - 1)
-    def _(layer):
-        ua[layer] = FINE_P[1] * ub[layer] + FINE_P[2] * applied(ub, layer)
-
-    @pl.loop(2, LT - 2)
-    def _(layer):
-        grow[layer] = FINE_P[0] * ub[layer] + applied(ua, layer)
-
     beside(1)
     sub_src, sub_dst = nat.at[1, own], nat.at[3, own]
     sub = remote(sub_src, sub_dst, sub_sem.at[0], sub_sem.at[1], device((k + 7) % 8, q))
@@ -285,19 +264,43 @@
     pl.when(has_cl)(lambda: to_cl.start())
     pl.when(has_cr)(lambda: to_cr.start())
 
-    @pl.loop(H, H + B)
-    def _(layer):
+    halo_arrived(0)
+    edges(has_l, 0, fill_con, blank_con)
+    edges(has_r, H + B, fill_con, blank_con)
+
+    each(H, H + B, fill_src, 4)
+
+    halo_arrived(2)
+    edges(has_l, 0, fill_src, blank_src)
+    edges(has_r, H + B, fill_src, blank_src)
+
+    def applied(ref, layer):
+        centre = ref[layer]
+        return kap[3, layer] * (6.0 * centre - neighbours(ref[layer - 1], centre, ref[layer + 1], mk))
+
+    def first_power(layer):
+        ua[layer] = FINE_P[1] * ub[layer] + FINE_P[2] * applied(ub, layer)
+
+    def second_power(layer):
+        grow[layer] = FINE_P[0] * ub[layer] + applied(ua, layer)
+
+    each(1, LT - 1, first_power, (LT - 2) // 2)
+    each(2, LT - 2, second_power, (LT - 4) // 2)
+
+    def fill_entry(layer):
         ua[layer] = natural(nat.at[1], layer)
 
-    halo_arrived(1)
-    for side, has, first in ((0, has_l, 0), (1, has_r, H + B)):
-        def fill(layer, side=side, first=first):
+    each(H, H + B, fill_entry, 4)
+
+    def entry_halo(side, has, first, sem):
+        def fill(layer):
             land[0, side, layer - first] = natural(nat.at[1], layer)
 
-        def blank(layer, side=side, first=first):
+        def blank(layer):
             land[0, side, layer - first] = nothing
             land[1, side, layer - first] = nothing
 
+        pl.when(has)(lambda: arrived(nat.at[1, pl.ds(first, H)], sem))
         edges(has, first, fill, blank)
 
     arrived(prof.at[1 - m], prof_sem.at[1])
@@ -354,6 +357,9 @@
         c_, d_ = state_copies(g + 1)
         last = COARSEN * SWEEPS // H
 
+        if with_source:
+            pl.when(g == 0)(lambda: entry_halo(0, has_l, 0, nat_recv.at[1, 1]))
+
         @pl.when(jnp.logical_and(g > 0, has_l))
         def _():
             b.wait_recv()
@@ -363,6 +369,9 @@
         @pl.when(jnp.logical_and((g + 1) % last != 0, has_l))
         def _():
             c_.start()
+
+        if with_source:
+            pl.when(g == 0)(lambda: entry_halo(1, has_r, H + B, nat_recv.at[0, 1]))
 
         @pl.when(jnp.logical_and(g > 0, has_r))
         def _():
@@ -390,21 +399,19 @@
         ua[layer] = value
         return value
 
-    @pl.loop(0, H)
-    def _(i):
+    def difference_l(i):
         stage[GROUPS % 2, 0, i] = difference(H + i)
 
+    each(0, H, difference_l, 3)
+
     pl.when(has_l)(lambda: first_copies[0].start())
 
-    @pl.loop(2 * H, B)
-    def _(layer):
-        difference(layer)
-
-    @pl.loop(0, H)
-    def _(i):
+    def difference_r(i):
         stage[GROUPS % 2, 1, i] = difference(B + i)
 
+    each(0, H, difference_r, 3)
     pl.when(has_r)(lambda: first_copies[1].start())
+    each(2 * H, B, difference, B - 2 * H)
 
     after = (k + 1) % 8
     rel_args = [
@@ -422,8 +429,13 @@
     def _(g):
         group(g, False)
 
-    for args in res_args:
-        push(*args)
+    early = after < 4
+
+    def give_residual():
+        for args in res_args:
+            push(*args)
+
+    pl.when(early)(give_residual)
 
     con_local.wait()
     pl.when(has_cl)(lambda: to_cr.wait_recv())
@@ -467,6 +479,11 @@
         )
 
     over = remote(eb.at[1, pl.ds(CH, 4)], eb.at[1, pl.ds(CH, 4)], chain_send.at[2, 0], chain_recv.at[2, 0], (1, c))
+
+    @pl.when(m == 1)
+    def _():
+        pl.semaphore_wait(turn, 1)
+        pl.when(jnp.logical_not(early))(give_residual)
 
     @pl.loop(0, 4)
     def _(i):
@@ -510,6 +527,12 @@
         pl.when(jnp.logical_and(more, has_cl))(lambda: d.start())
         pl.when(jnp.logical_and(more, has_cr))(lambda: e.start())
         pl.when(jnp.logical_and(i == 3, m == 0))(lambda: over.start())
+
+        @pl.when(jnp.logical_and(i == 0, m == 0))
+        def _():
+            pl.semaphore_signal(turn, inc=1, device_id=(1, c), device_id_type=MESH)
+            pl.when(jnp.logical_not(early))(give_residual)
+
         arrived(rel_in.at[i], out_recv.at[0, i])
         for layer in range(4):
             out_rows(residual, i, layer, res_in[i, layer])
@@ -589,7 +612,7 @@
             dma((2,)), dma((5,)), dma((2,)),
             dma((2, 2)), dma((2, 2)),
             dma((2, 4)), dma((2, 4)),
-            dma((3, 2)), dma((3, 2)),
+            dma((3, 2)), dma((3, 2)), pltpu.SemaphoreType.REGULAR,
         ],
         compiler_params=pltpu.CompilerParams(
             collective_id=0, has_side_effects=True, vmem_limit_bytes=67043328

time: 137 us -> 130 us (0.949)
  Pallas kernels: 132 us -> 125 us
    pallas_call x1, Pallas kernels: 132 us -> 125 us  [body(): pl.pallas_call(kernel, name='mgrit', out_shape=(out, out), in_specs=[anys...]
where the time goes in v3:
time: 130 us
  Pallas kernels  125 us (96%)
  local copies, waits for them, and re-layouts  4.07 us (3%)
    pallas_call x1, Pallas kernels, body(): pl.pallas_call(kernel, name='mgrit', out_shape=(out, out), in_specs=[anys...  125 us
    unnamed x4, local copies, waits for them, and re-layouts  2.74 us

profile of v3, /device:TPU:31, one launch (start us, length us, event | category | flops | bytes accessed | tf_op | source)
XLA Modules:
  0.0 129.7 jit_solution(18013332363259337056)
XLA Ops:
  0.6 1.3 %broadcast_in_dim.2.amount = f32[32,128]{1,0:T(8,128)} broadcast(f32[32]{0:T(128)} %param.9), dimensions={0} | broadcast | bytes 16512 | tf_op jit(solution)/shard_map/broadcast_in_dim | solution.py:576
  2.0 125.0 %mgrit.1 = (f32[4,4,64,128]{3,2,1,0:T(8,128)}, f32[4,4,64,128]{3,2,1,0:T(8,128)}) custom-call(f32[4,64,128]{2,1,0:T(8,128)} %initial.1, f32[4,4,64,128]{3,2,1,0:T(8,128)} %guess.1, f32[4,64,128]{2,1,0:T(8,128)} %conduct.1, f32[4,64,128]{2,1,0:T(8,128)} %source.1, f32[32,128]{1,0:T(8,128)} %broadcast_in_dim.2.amount), custom_call_target="tpu_custom_call" | custom-call | tf_op jit(solution)/shard_map/mgrit/pallas_call | solution.py:585
  127.0 0.0 copy-start
  127.0 1.9 %copy.9 = f32[4,4,64,128]{3,2,1,0:T(8,128)} copy(f32[4,4,64,128]{3,2,1,0:T(8,128)} %get-tuple-element.4) | data formatting | bytes 1048576
  128.9 0.0 copy-done
  128.9 0.8 copy.10
Async XLA Ops:
  127.0 2.0 %copy-start = (f32[4,4,64,128]{3,2,1,0:T(8,128)S(1)}, f32[4,4,64,128]{3,2,1,0:T(8,128)}, u32[]{:S(2)}) copy-start(f32[4,4,64,128]{3,2,1,0:T(8,128)} %get-tuple-element.5) | copy-start | bytes 1572868

commit v4 on v3

--- a/solution.py
+++ b/solution.py
@@ -79,7 +79,7 @@
     corrected, residual,
     nat, con_nat, prof, kap, mul, grow, ua, ub, land, stage, rel, kc, mc, eb, t1, t2, res_in, rel_in,
     in_send, in_recv, nat_send, nat_recv, prof_sem, con_sem, sub_sem, halo_send, halo_recv,
-    out_send, out_recv, chain_send, chain_recv, turn,
+    out_send, out_recv, chain_send, chain_recv, fin, fin_sem, turn,
 ):
     m = lax.axis_index("tm")
     c = lax.axis_index("space")
@@ -165,7 +165,7 @@
     to_cr = remote(conduct.at[pl.ds(1, CH)], con_nat.at[pl.ds(0, CH)], con_sem.at[3], con_sem.at[4], chain_right)
 
     partner = (1 - m, c)
-    to_partner = remote(amount, prof.at[m], prof_sem.at[0], prof_sem.at[1], partner)
+    to_partner = remote(prof.at[m], prof.at[m], prof_sem.at[0], prof_sem.at[1], partner)
 
     give(0, 0, conduct, x + 4 * m)
     give(2, 0, source, x + 4 * m)
@@ -182,7 +182,8 @@
     for i in range(3):
         give(1, i, guess.at[i], 4 * m + i + 1)
     give(1, 3, guess.at[3], 4, m == 0)
-    prof[m] = amount[...]
+    for t in range(4 * COARSEN):
+        prof[m, pl.ds(t, 1), :] = jnp.full((1, 128), amount[t], F32)
 
     nat_copies = []
 
@@ -478,6 +479,9 @@
             remote(eb.at[p, pl.ds(4, CH)], eb.at[p, pl.ds(0, CH)], chain_send.at[1, p], chain_recv.at[1, p], rgt),
         )
 
+    def result(n, i):
+        return pltpu.make_async_copy(fin.at[n, i], (corrected, residual)[n].at[i], fin_sem.at[n, i])
+
     over = remote(eb.at[1, pl.ds(CH, 4)], eb.at[1, pl.ds(CH, 4)], chain_send.at[2, 0], chain_recv.at[2, 0], (1, c))
 
     @pl.when(m == 1)
@@ -535,9 +539,15 @@
 
         arrived(rel_in.at[i], out_recv.at[0, i])
         for layer in range(4):
-            out_rows(residual, i, layer, res_in[i, layer])
-            out_rows(corrected, i, layer, rel_in[i, layer] + eb[p, CH + layer])
-
+            out_rows(fin.at[0], i, layer, rel_in[i, layer] + eb[p, CH + layer])
+        result(0, i).start()
+        for layer in range(4):
+            out_rows(fin.at[1], i, layer, res_in[i, layer])
+        result(1, i).start()
+
+    for i in range(4):
+        for n in range(2):
+            result(n, i).wait()
     d, e = chain_copies(2)
     pl.when(has_cl)(lambda: d.wait_send())
     pl.when(has_cr)(lambda: e.wait_send())
@@ -573,9 +583,7 @@
 
 
 def body(initial, guess, conduct, source, profile):
-    amount = jnp.broadcast_to(profile[:, None], (4 * COARSEN, 128))
     anyspace = pl.BlockSpec(memory_space=pl.ANY)
-    vmem = pl.BlockSpec(memory_space=pltpu.VMEM)
     out = jax.ShapeDtypeStruct((4, 4, 64, 128), F32)
     dma = pltpu.SemaphoreType.DMA
 
@@ -586,8 +594,8 @@
         kernel,
         name="mgrit",
         out_shape=(out, out),
-        in_specs=[anyspace, anyspace, anyspace, anyspace, vmem],
-        out_specs=(vmem, vmem),
+        in_specs=[anyspace, anyspace, anyspace, anyspace, pl.BlockSpec(memory_space=pltpu.SMEM)],
+        out_specs=(anyspace, anyspace),
         scratch_shapes=[
             pltpu.VMEM((4, LT, 64, 128), F32),
             pltpu.VMEM((CT, 64, 128), F32),
@@ -612,12 +620,14 @@
             dma((2,)), dma((5,)), dma((2,)),
             dma((2, 2)), dma((2, 2)),
             dma((2, 4)), dma((2, 4)),
-            dma((3, 2)), dma((3, 2)), pltpu.SemaphoreType.REGULAR,
+            dma((3, 2)), dma((3, 2)),
+            pltpu.VMEM((2, 4, 4, 64, 128), F32),
+            dma((2, 4)), pltpu.SemaphoreType.REGULAR,
         ],
         compiler_params=pltpu.CompilerParams(
             collective_id=0, has_side_effects=True, vmem_limit_bytes=67043328
         ),
-    )(initial, guess, conduct, source, amount)
+    )(initial, guess, conduct, source, profile)
 
 
 def solution(mesh):

time: 130 us -> 130 us (level); the launches traced: 130 us -> 128 us
  local copies, waits for them, and re-layouts: 4.07 us -> 2.74 us
    broadcast_in_dim x1 -> x0, local copies, waits for them, and re-layouts: 1.33 us -> none  [body(): amount = jnp.broadcast_to(profile[:, None], (4 * COARSEN, 128))]
where the time goes in v4:
time: 130 us; the launch traced here: 128 us
  Pallas kernels  125 us (96%)
  local copies, waits for them, and re-layouts  2.74 us (2%)
    pallas_call x1, Pallas kernels, body(): pl.pallas_call(kernel, name='mgrit', out_shape=(out, out), in_specs=[anys...  125 us
    unnamed x4, local copies, waits for them, and re-layouts  2.74 us

profile of v4, /device:TPU:31, one launch (start us, length us, event | category | flops | bytes accessed | tf_op | source)
XLA Modules:
  0.0 128.2 jit_solution(13212287507222773720)
XLA Ops:
  0.6 124.9 %mgrit.1 = (f32[4,4,64,128]{3,2,1,0:T(8,128)}, f32[4,4,64,128]{3,2,1,0:T(8,128)}) custom-call(f32[4,64,128]{2,1,0:T(8,128)} %initial.1, f32[4,4,64,128]{3,2,1,0:T(8,128)} %guess.1, f32[4,64,128]{2,1,0:T(8,128)} %conduct.1, f32[4,64,128]{2,1,0:T(8,128)} %source.1, f32[32]{0:T(128)} %amount.1), custom_call_target="tpu_custom_call" | custom-call | tf_op jit(solution)/shard_map/mgrit/pallas_call | solution.py:593
  125.5 0.0 copy-start
  125.5 1.9 %copy.9 = f32[4,4,64,128]{3,2,1,0:T(8,128)} copy(f32[4,4,64,128]{3,2,1,0:T(8,128)} %get-tuple-element.4) | data formatting | bytes 1048576
  127.5 0.0 copy-done
  127.5 0.8 copy.10
Async XLA Ops:
  125.5 2.0 %copy-start = (f32[4,4,64,128]{3,2,1,0:T(8,128)S(1)}, f32[4,4,64,128]{3,2,1,0:T(8,128)}, u32[]{:S(2)}) copy-start(f32[4,4,64,128]{3,2,1,0:T(8,128)} %get-tuple-element.5) | copy-start | bytes 1572868

commit v5 on v4

--- a/solution.py
+++ b/solution.py
@@ -173,7 +173,7 @@
     for array in (0, 2):
         column = nat.at[array, pl.ds(H + 4 * x, 4)]
         relays[array] = [
-            remote(column, column, in_send.at[array, d], in_recv.at[array, x], (m, 16 * z + 4 * y + (x + d) % 4)) for d in range(1, 4)
+            remote(column, column, in_send.at[array, d], in_recv.at[array, x], (m, 16 * z + 4 * y + (x + d) % 4)) for d in (3, 1, 2)
         ]
         arrived(column, in_recv.at[array, x])
         for relay in relays[array]:

time: 130 us -> 128 us (0.985); the launches traced: 128 us -> 128 us
  no operation moved by 1% of the time
where the time goes in v5:
time: 128 us
  Pallas kernels  125 us (98%)
  local copies, waits for them, and re-layouts  2.74 us (2%)
    pallas_call x1, Pallas kernels, body(): pl.pallas_call(kernel, name='mgrit', out_shape=(out, out), in_specs=[anys...  125 us
    unnamed x4, local copies, waits for them, and re-layouts  2.74 us

profile of v5, /device:TPU:31, one launch (start us, length us, event | category | flops | bytes accessed | tf_op | source)
XLA Modules:
  0.0 128.0 jit_solution(12093472121652524452)
XLA Ops:
  0.6 124.6 %mgrit.1 = (f32[4,4,64,128]{3,2,1,0:T(8,128)}, f32[4,4,64,128]{3,2,1,0:T(8,128)}) custom-call(f32[4,64,128]{2,1,0:T(8,128)} %initial.1, f32[4,4,64,128]{3,2,1,0:T(8,128)} %guess.1, f32[4,64,128]{2,1,0:T(8,128)} %conduct.1, f32[4,64,128]{2,1,0:T(8,128)} %source.1, f32[32]{0:T(128)} %amount.1), custom_call_target="tpu_custom_call" | custom-call | tf_op jit(solution)/shard_map/mgrit/pallas_call | solution.py:593
  125.2 0.0 copy-start
  125.2 1.9 %copy.9 = f32[4,4,64,128]{3,2,1,0:T(8,128)} copy(f32[4,4,64,128]{3,2,1,0:T(8,128)} %get-tuple-element.4) | data formatting | bytes 1048576
  127.2 0.0 copy-done
  127.2 0.8 copy.10
Async XLA Ops:
  125.2 2.0 %copy-start = (f32[4,4,64,128]{3,2,1,0:T(8,128)S(1)}, f32[4,4,64,128]{3,2,1,0:T(8,128)}, u32[]{:S(2)}) copy-start(f32[4,4,64,128]{3,2,1,0:T(8,128)} %get-tuple-element.5) | copy-start | bytes 1572868
